TPU v7x, 32 devices: a whole 2x2x4 slice. The times are simulated.
32 devices in a mesh: rep: 4 (over x, core), ep: 4 (over z), grp: 2 (over y).
Axes of the slice: x: 2, y: 2, z: 4, core: 2. Of those that a mesh axis runs over, the one named last changes fastest.
Arguments:
- tokens: bfloat16 [4096, 2048], P(('rep', 'ep', 'grp')), may hold values from -6 to 6
- grad_out: bfloat16 [4096, 2048], P(('rep', 'ep', 'grp')), may hold values from -6 to 6
- expert_ids: int32 [4096, 2], P(('rep', 'ep', 'grp')), may hold values from 0 to 7, as said below
- combine: bfloat16 [4096, 2], P(('rep', 'ep', 'grp')), may hold values from 0.099609375 to 1
- weights: bfloat16 [2048, 3, 7168], P('grp', None, 'ep'), may hold values from -0.125 to 0.125
Outputs:
- grad_tokens: bfloat16 [4096, 2048], P(('rep', 'ep', 'grp'))
- grad_combine: float32 [4096, 2], P(('rep', 'ep', 'grp'))
- grad_weights: float32 [2048, 3, 7168], P(('rep', 'grp'), None, 'ep')
Inputs may be any that keep to these rules, and one draw needn't show every extreme that they name: `expert_ids`: each token names 2 different experts, at most one of them below 1. No expert below 1 is named by more than 4 tokens of one device, and each of them is named by exactly 4 tokens of some device.
All inputs are finite; a program needn't handle non-finite values.
Results may differ from a plain program's by a relative error of at most 0.0085.
Values may be sent and summed in bfloat16 or wider, within the bound.
A program may use at most 128 MiB of HBM per device.

v0:
```python
import jax
import jax.numpy as jnp
from jax import lax
from jax.sharding import PartitionSpec as P

FLIGHT = 1
CAP = 4


def route_slots(routing, gate_vals):
    match = (routing == 0).astype(jnp.float32)
    assigned = jnp.sum(match, axis=1)
    combined = jnp.sum(match * gate_vals.astype(jnp.float32), axis=1)
    before = jnp.cumsum(assigned) - assigned
    slot_index = jnp.arange(CAP, dtype=jnp.float32)
    slot_map = (before[None, :] == slot_index[:, None]).astype(jnp.float32) * assigned[None, :]
    return (match, combined, slot_map)


def local(tokens, grad_out, expert_ids, combine, weights):
    ep, rep, grp = (lax.axis_size("ep"), lax.axis_size("rep"), lax.axis_size("grp"))
    me_g = lax.axis_index("grp")
    width = tokens.shape[1]
    half = width // grp
    owner = width // (rep * grp)
    hid = weights.shape[2]
    peers = ep * grp
    rows = peers * CAP
    pad = 128
    f32, bf16 = (jnp.float32, jnp.bfloat16)
    match, combined, slot_map = route_slots(expert_ids, combine)
    slot_bf = slot_map.astype(bf16)
    xs = jnp.dot(slot_bf, tokens, preferred_element_type=f32).astype(bf16)
    ys = jnp.dot(slot_bf, grad_out, preferred_element_type=f32).astype(bf16)
    cs = jnp.sum(slot_map * combined[None, :], axis=1).astype(bf16)
    sent = jnp.concatenate([xs, ys, jnp.broadcast_to(cs[:, None], (CAP, pad))], axis=1)
    got = lax.all_gather(sent, ("grp", "ep"), axis=0, tiled=True)
    pair = got[:, : 2 * width].reshape(rows, 2, width)
    scale = got[:, 2 * width : 2 * width + 1].astype(f32)
    mine = lax.dynamic_slice_in_dim(pair, me_g * half, half, axis=2)
    blocks = pair.reshape(rows, 2, rep, grp, owner)
    blocks = lax.dynamic_index_in_dim(blocks, me_g, axis=3, keepdims=False)
    blocks = jnp.transpose(blocks, (2, 0, 1, 3)).reshape(rep, rows, 2 * owner)
    cols = lax.all_to_all(blocks, "rep", split_axis=0, concat_axis=0, tiled=True)
    cols = cols.reshape(rep * rows, 2, owner)
    w = jnp.transpose(weights, (1, 0, 2))
    pre = jnp.concatenate(
        [
            jnp.dot(mine[:, 0], w[0], preferred_element_type=f32),
            jnp.dot(mine[:, 0], w[1], preferred_element_type=f32),
            jnp.dot(mine[:, 1], w[2], preferred_element_type=f32),
        ],
        axis=1,
    )
    pre = lax.psum(pre, "grp")
    a, b, back = (pre[:, :hid], pre[:, hid : 2 * hid], pre[:, 2 * hid :])
    sig = jax.nn.sigmoid(a)
    act = a * sig
    h = act * b
    dh = scale * back
    da = (dh * b * sig * (1.0 + a * (1.0 - sig))).astype(bf16)
    db = (dh * act).astype(bf16)
    hc = (scale * h).astype(bf16)
    pc = jnp.sum(h * back, axis=1, keepdims=True).astype(bf16)
    hidden = lax.all_gather(jnp.concatenate([da, db, hc], axis=1), "rep", axis=0, tiled=True)
    dn = (((1,), (1,)), ((), ()))
    px = lax.dot_general(da, w[0], dn, preferred_element_type=f32)
    px = (px + lax.dot_general(db, w[1], dn, preferred_element_type=f32)).astype(bf16)
    out = jnp.concatenate([px, jnp.broadcast_to(pc, (rows, pad))], axis=1)
    ret = lax.all_to_all(out, ("grp", "ep"), split_axis=0, concat_axis=0, tiled=True)
    ret = ret.reshape(grp, ep, CAP, half + pad).astype(f32)
    summed = jnp.sum(ret, axis=1)
    summed_x = jnp.transpose(summed[:, :, :half], (1, 0, 2)).reshape(CAP, width)
    summed_c = summed[0, :, half]
    highest = lax.Precision.HIGHEST
    tn = (((0,), (0,)), ((), ()))
    grad_tokens = lax.dot_general(slot_map, summed_x, tn, precision=highest).astype(bf16)
    per_token = jnp.sum(slot_map * summed_c[:, None], axis=0)
    grad_combine = match * per_token[:, None]
    gw = [
        lax.dot_general(
            cols[:, i], hidden[:, k * hid : (k + 1) * hid], tn, preferred_element_type=f32
        )
        for k, i in ((0, 0), (1, 0), (2, 1))
    ]
    return (grad_tokens, grad_combine, jnp.stack(gw, axis=1))


def solution(mesh):
    split = P(("rep", "ep", "grp"), None)
    in_specs = (split, split, split, split, P("grp", None, "ep"))
    out_specs = (split, split, P(("rep", "grp"), None, "ep"))
    return jax.shard_map(local, mesh=mesh, in_specs=in_specs, out_specs=out_specs, check_vma=False)
```

profile of v0, /device:TPU:0, one launch (start us, length us, event | category | flops | bytes accessed | tf_op | source)
XLA Modules:
  0.0 131.9 jit_solution(17238979611261452542)
XLA Ops:
  7.2 0.0 copy-start
  7.2 0.0 all-reduce.2.cloned.1.call-start
  7.2 0.7 convert_reduce_fusion.2
  8.0 0.1 copy.35
  8.1 0.2 reduce-window.8
  8.3 0.1 reduce
  8.4 0.1 fusion.18
  8.5 0.0 copy-done
  8.5 0.2 convolution_convert_fusion.1
  8.7 1.2 convolution_convert_fusion.2
  9.9 0.1 broadcast_in_dim.4
  10.0 32.9 %all-gather = bf16[8,4,4224]{2,1,0:T(4,128)(2,1)S(1)} all-gather(bf16[1,4,4224]{2,1,0:T(4,128)(2,1)S(1)} %maximum_bitcast_fusion), channel_id=1, replica_groups=mesh['rep'=4,'ep'=4,'grp'=2] {'grp','ep'}, dimensions={0}, use_global_device_ids=true | all-gather | bytes 304128 | tf_op jit(solution)/shard_map/all_gather | solution.py:37
  42.9 0.1 reshape.73
  43.0 0.2 reshape.66
  43.2 0.3 constant_dynamic-slice_fusion
  43.5 2.7 %fusion.2 = f32[32,1792]{1,0:T(8,128)S(1)} fusion(bf16[3,1024,1792]{2,1,0:T(8,128)(2,1)} %bitcast.58, bf16[32,1,1024]{2,1,0:T(2,128)(2,1)S(1)} %get-tuple-element.9), kind=kOutput, calls=%fused_computation.6 | convolution fusion | flops 117440512 | bytes 3964928 | tf_op jit(solution)/shard_map/dot_general | solution.py:49
  46.3 2.7 %fusion.4 = f32[32,1792]{1,0:T(8,128)S(1)} fusion(bf16[3,1024,1792]{2,1,0:T(8,128)(2,1)} %bitcast.59, bf16[32,1,1024]{2,1,0:T(2,128)(2,1)S(1)} %get-tuple-element.9), kind=kOutput, calls=%fused_computation.8 | convolution fusion | flops 117440512 | bytes 3964928 | tf_op jit(solution)/shard_map/dot_general | solution.py:50
  49.0 2.8 %fusion = f32[32,1792]{1,0:T(8,128)S(1)} fusion(bf16[3,1024,1792]{2,1,0:T(8,128)(2,1)} %bitcast.60, bf16[32,1,1024]{2,1,0:T(2,128)(2,1)S(1)} %get-tuple-element.10), kind=kOutput, calls=%fused_computation.2 | convolution fusion | flops 117440512 | bytes 3964928 | tf_op jit(solution)/shard_map/dot_general | solution.py:51
  51.8 0.9 pad_maximum_fusion.1
  52.7 0.0 all-reduce.2.cloned.1.call-update
  52.7 0.0 all-gather.3.cloned.1.call-start
  52.7 0.2 reshape_reshape.3
  52.9 0.1 convert_reduce_fusion.1
  53.0 33.3 %all-reduce.2.cloned.1.call-done = f32[32,5376]{1,0:T(8,128)} async-done(((f32[32,5376]{1,0:T(8,128)}), f32[32,5376]{1,0:T(8,128)}) %all-reduce.2.cloned.1.call-update) | async-done | bytes 688144 | tf_op jit(solution)/shard_map/psum | solution.py:55
  86.3 1.4 %multiply_convert_fusion = (bf16[32,1792]{1,0:T(8,128)(2,1)S(1)}, bf16[32,1792]{1,0:T(8,128)(2,1)S(1)}, bf16[32,1792]{1,0:T(8,128)(2,1)S(1)}, bf16[32]{0:T(256)(128)(2,1)S(1)}) fusion(f32[32]{0:T(128)S(1)} %convert_reduce_fusion.1, f32[32,5376]{1,0:T(8,128)} %all-reduce.2.cloned.1.call-done), kind=kLoop, calls=%fused_computation.22 | loop fusion | flops 1089504 | bytes 1032384 | tf_op jit(solution)/shard_map/convert_element_type | solution.py:63
  87.7 0.8 pad_maximum_fusion.2
  88.5 0.0 all-gather.3.cloned.1.call-update
  88.5 0.3 constant_dynamic-slice_fusion.1
  88.8 0.1 copy.63
  88.9 7.1 %all_to_all.14 = bf16[4,32,512]{2,1,0:T(8,128)(2,1)S(1)} all-to-all(bf16[4,32,512]{2,1,0:T(8,128)(2,1)S(1)} %bitcast.64), channel_id=1, replica_groups=mesh['rep'=4,'ep'=4,'grp'=2] {'rep'}, dimensions={0} | all-to-all | bytes 262144 | tf_op jit(solution)/shard_map/all_to_all | solution.py:44
  96.1 0.0 copy-start.1
  96.1 3.2 %fusion.1 = f32[32,1024]{1,0:T(8,128)S(1)} fusion(bf16[32,1792]{1,0:T(8,128)(2,1)S(1)} %get-tuple-element.7, bf16[3,1024,1792]{2,1,0:T(8,128)(2,1)} %bitcast.61), kind=kOutput, calls=%fused_computation.5 | convolution fusion | flops 117440512 | bytes 3915776 | tf_op jit(solution)/shard_map/dot_general | solution.py:67
  99.3 3.2 %fusion.6 = bf16[32,1024]{1,0:T(8,128)(2,1)S(1)} fusion(f32[32,1024]{1,0:T(8,128)S(1)} %fusion.1, bf16[32,1792]{1,0:T(8,128)(2,1)S(1)} %get-tuple-element.6, bf16[3,1024,1792]{2,1,0:T(8,128)(2,1)} %bitcast.62), kind=kOutput, calls=%fused_computation.16 | convolution fusion | flops 117506048 | bytes 3981312 | tf_op jit(solution)/shard_map/dot_general | solution.py:68
  102.6 0.1 broadcast_in_dim.5
  102.7 0.7 all_to_all.9
  103.3 4.9 %all-to-all-start = ((bf16[8,4,1152]{2,1,0:T(4,128)(2,1)}), bf16[8,4,1152]{2,1,0:T(4,128)(2,1)S(1)}, u32[]{:S(2)}, u32[]{:S(2)}) async-start(bf16[8,4,1152]{2,1,0:T(4,128)(2,1)} %all_to_all.9), calls=%async_computation | async-start | bytes 147456 | tf_op jit(solution)/shard_map/all_to_all | solution.py:70
  108.2 0.2 fusion.32
  108.4 6.9 %all-to-all-done = bf16[8,4,1152]{2,1,0:T(4,128)(2,1)S(1)} async-done(((bf16[8,4,1152]{2,1,0:T(4,128)(2,1)}), bf16[8,4,1152]{2,1,0:T(4,128)(2,1)S(1)}, u32[]{:S(2)}, u32[]{:S(2)}) %all-to-all-start) | async-done | bytes 73760 | tf_op jit(solution)/shard_map/all_to_all | solution.py:70
  115.3 0.1 slice_reduce_fusion
  115.4 0.1 fusion.19
  115.5 0.0 copy-done.1
  115.5 0.6 broadcast_select_fusion
  116.1 1.8 %convolution_convert_fusion = bf16[128,2048]{1,0:T(8,128)(2,1)} fusion(f32[4,2048]{1,0:T(4,128)S(1)} %bitcast.65, f32[128]{0:T(128)S(1)} %get-tuple-element.3, f32[128]{0:T(128)S(1)} %sub.10), kind=kOutput, calls=%fused_computation.12 | convolution fusion | flops 12846080 | bytes 558080 | tf_op jit(solution)/shard_map/dot_general | solution.py:77
  117.9 0.0 all-gather.3.cloned.1.call-done
  117.9 1.4 %convolution_bitcast_fusion.1 = f32[256,1,1792]{2,0,1:T(8,128)S(1)} fusion(bf16[128,5376]{1,0:T(8,128)(2,1)} %all-gather.3.cloned.1.call-done, bf16[128,1,256]{2,1,0:T(2,128)(2,1)S(1)} %get-tuple-element.11), kind=kOutput, calls=%fused_computation.10 | convolution fusion | flops 117440512 | bytes 2359296 | tf_op jit(solution)/shard_map/dot_general | solution.py:81
  119.4 1.4 %convolution_bitcast_fusion.2 = f32[256,1,1792]{2,0,1:T(8,128)S(1)} fusion(bf16[128,5376]{1,0:T(8,128)(2,1)} %all-gather.3.cloned.1.call-done, bf16[128,1,256]{2,1,0:T(2,128)(2,1)S(1)} %get-tuple-element.11), kind=kOutput, calls=%fused_computation.11 | convolution fusion | flops 117440512 | bytes 2359296 | tf_op jit(solution)/shard_map/dot_general | solution.py:81
  120.8 1.4 %convolution_bitcast_fusion = f32[256,1,1792]{2,0,1:T(8,128)S(1)} fusion(bf16[128,5376]{1,0:T(8,128)(2,1)} %all-gather.3.cloned.1.call-done, bf16[128,1,256]{2,1,0:T(2,128)(2,1)S(1)} %get-tuple-element.12), kind=kOutput, calls=%fused_computation.9 | convolution fusion | flops 117440512 | bytes 2359296 | tf_op jit(solution)/shard_map/dot_general | solution.py:81
  122.2 2.8 %pad_maximum_fusion = f32[256,3,1792]{2,0,1:T(8,128)} fusion(f32[256,1,1792]{2,0,1:T(8,128)S(1)} %convolution_bitcast_fusion, f32[256,1,1792]{2,0,1:T(8,128)S(1)} %convolution_bitcast_fusion.1, f32[256,1,1792]{2,0,1:T(8,128)S(1)} %convolution_bitcast_fusion.2), kind=kLoop, calls=%fused_computation | loop fusion | flops 2752512 | bytes 11010048 | tf_op jit(solution)/shard_map/stack | solution.py:86
  (8 shorter events, 0.1 us)
Async XLA Ops:
  7.2 1.3 %copy-start = (bf16[128,2048]{1,0:T(8,128)(2,1)S(1)}, bf16[128,2048]{1,0:T(8,128)(2,1)}, u32[]{:S(2)}) copy-start(bf16[128,2048]{1,0:T(8,128)(2,1)} %param.6) | copy-start | bytes 1572868
  7.2 79.1 %all-reduce.2.cloned.1.call-start = ((), (), s32[]{:S(2)}) async-start(), calls=%async_computation.2 | async-start | bytes 1376256 | tf_op jit(solution)/shard_map/psum | solution.py:55
  52.7 65.2 %all-gather.3.cloned.1.call-start = ((), (), s32[]{:S(2)}) async-start(), calls=%async_computation.3 | async-start | bytes 1720320 | tf_op jit(solution)/shard_map/all_gather | solution.py:65
  96.1 19.4 %copy-start.1 = (s32[128,2]{0,1:T(2,128)S(1)}, s32[128,2]{0,1:T(2,128)}, u32[]{:S(2)}) copy-start(s32[128,2]{0,1:T(2,128)} %param.7) | copy-start | bytes 3076
  103.3 11.9 %all-to-all-start = ((bf16[8,4,1152]{2,1,0:T(4,128)(2,1)}), bf16[8,4,1152]{2,1,0:T(4,128)(2,1)S(1)}, u32[]{:S(2)}, u32[]{:S(2)}) async-start(bf16[8,4,1152]{2,1,0:T(4,128)(2,1)} %all_to_all.9), calls=%async_computation | async-start | bytes 147456 | tf_op jit(solution)/shard_map/all_to_all | solution.py:70
Sparse Core Ops, SparseCore 0:
  52.8 33.4 all-reduce.1
  88.7 18.5 all-gather.2
where the time goes:
time: 133 us; the launch traced here: 132 us
  waiting for transfers between devices  40.2 us (30%)
  blocking collectives  40 us (30%)
  matrix products  22.3 us (17%)
  between operations  14.2 us (11%)
  other arithmetic  7.88 us (6%)
  starting transfers between devices  4.95 us (4%)
  local copies, waits for them, and re-layouts  2.39 us (2%)
    psum x1, waiting for transfers between devices, local(): pre = lax.psum(pre, 'grp')  33.3 us
    all_gather x1, blocking collectives, local(): got = lax.all_gather(sent, ('grp', 'ep'), axis=0, tiled=True)  32.9 us
    all_to_all x1, blocking collectives, local(): lax.all_to_all(blocks, 'rep', split_axis=0, concat_axis=0, tiled=True)  7.14 us
    all_to_all x1, waiting for transfers between devices, local(): lax.all_to_all(out, ('grp', 'ep'), split_axis=0, concat_axis=0, tiled=True)  6.87 us
    all_to_all x1, starting transfers between devices, local(): lax.all_to_all(out, ('grp', 'ep'), split_axis=0, concat_axis=0, tiled=True)  4.87 us
    dot_general x3, matrix products, local(): lax.dot_general(cols[:, i], hidden[:, k * hid:(k + 1) * hid], tn, preferr...  4.31 us
    dot_general x1, matrix products, local(): lax.dot_general(db, w[1], dn, preferred_element_type=f32)  3.24 us
    dot_general x1, matrix products, local(): px = lax.dot_general(da, w[0], dn, preferred_element_type=f32)  3.21 us
  transfers between devices with their start and end apart: 3, of which 2 were waited for; matrix products, arithmetic and copies ran while one was open for 8% of the time, Pallas kernels for 0%

commit v1 on v0

--- a/solution.py
+++ b/solution.py
@@ -52,7 +52,8 @@
         ],
         axis=1,
     )
-    pre = lax.psum(pre, "grp")
+    pieces = lax.all_gather(pre, "grp", axis=0, tiled=False)
+    pre = pieces.sum(axis=0)
     a, b, back = (pre[:, :hid], pre[:, hid : 2 * hid], pre[:, 2 * hid :])
     sig = jax.nn.sigmoid(a)
     act = a * sig

time: 133 us -> 126 us (0.947)
  waiting for transfers between devices: 40.2 us -> 32.9 us
    psum x1 -> x0, waiting for transfers between devices: 33.3 us -> none  [local(): pre = lax.psum(pre, 'grp')]
    all_gather x0 -> x1, waiting for transfers between devices: none -> 26 us  [local(): pieces = lax.all_gather(pre, 'grp', axis=0, tiled=False)]
    reduce_sum x0 -> x1, other arithmetic: none -> 1.49 us  [local(): pre = pieces.sum(axis=0)]
where the time goes in v1:
time: 126 us; the launch traced here: 125 us
  blocking collectives  40 us (32%)
  waiting for transfers between devices  32.9 us (26%)
  matrix products  22.3 us (18%)
  between operations  14.2 us (11%)
  other arithmetic  8.16 us (6%)
  starting transfers between devices  4.95 us (4%)
  local copies, waits for them, and re-layouts  2.39 us (2%)
    all_gather x1, blocking collectives, local(): got = lax.all_gather(sent, ('grp', 'ep'), axis=0, tiled=True)  32.9 us
    all_gather x1, waiting for transfers between devices, local(): pieces = lax.all_gather(pre, 'grp', axis=0, tiled=False)  26 us
    all_to_all x1, blocking collectives, local(): lax.all_to_all(blocks, 'rep', split_axis=0, concat_axis=0, tiled=True)  7.14 us
    all_to_all x1, waiting for transfers between devices, local(): lax.all_to_all(out, ('grp', 'ep'), split_axis=0, concat_axis=0, tiled=True)  6.87 us
    all_to_all x1, starting transfers between devices, local(): lax.all_to_all(out, ('grp', 'ep'), split_axis=0, concat_axis=0, tiled=True)  4.87 us
    dot_general x3, matrix products, local(): lax.dot_general(cols[:, i], hidden[:, k * hid:(k + 1) * hid], tn, preferr...  4.31 us
    dot_general x1, matrix products, local(): lax.dot_general(db, w[1], dn, preferred_element_type=f32)  3.24 us
    dot_general x1, matrix products, local(): px = lax.dot_general(da, w[0], dn, preferred_element_type=f32)  3.21 us
  transfers between devices with their start and end apart: 3, of which 2 were waited for; matrix products, arithmetic and copies ran while one was open for 8% of the time, Pallas kernels for 0%

profile of v1, /device:TPU:0, one launch (start us, length us, event | category | flops | bytes accessed | tf_op | source)
XLA Modules:
  0.0 124.9 jit_solution(2781036931998152221)
XLA Ops:
  7.2 0.0 copy-start
  7.2 0.0 all-gather.7.cloned.1.call-start
  7.2 0.7 convert_reduce_fusion.2
  8.0 0.1 copy.35
  8.1 0.2 reduce-window.8
  8.3 0.1 reduce
  8.4 0.1 fusion.18
  8.5 0.0 copy-done
  8.5 0.2 convolution_convert_fusion.1
  8.7 1.2 convolution_convert_fusion.2
  9.9 0.1 broadcast_in_dim.4
  10.0 32.9 %all-gather.1 = bf16[8,4,4224]{2,1,0:T(4,128)(2,1)S(1)} all-gather(bf16[1,4,4224]{2,1,0:T(4,128)(2,1)S(1)} %maximum_bitcast_fusion), channel_id=1, replica_groups=mesh['rep'=4,'ep'=4,'grp'=2] {'grp','ep'}, dimensions={0}, use_global_device_ids=true | all-gather | bytes 304128 | tf_op jit(solution)/shard_map/all_gather | solution.py:37
  42.9 0.1 reshape.74
  43.0 0.2 reshape.66
  43.2 0.3 constant_dynamic-slice_fusion
  43.5 2.7 %fusion.2 = f32[32,1792]{1,0:T(8,128)S(1)} fusion(bf16[3,1024,1792]{2,1,0:T(8,128)(2,1)} %bitcast.59, bf16[32,1,1024]{2,1,0:T(2,128)(2,1)S(1)} %get-tuple-element.9), kind=kOutput, calls=%fused_computation.6 | convolution fusion | flops 117440512 | bytes 3964928 | tf_op jit(solution)/shard_map/dot_general | solution.py:49
  46.3 2.7 %fusion.4 = f32[32,1792]{1,0:T(8,128)S(1)} fusion(bf16[3,1024,1792]{2,1,0:T(8,128)(2,1)} %bitcast.60, bf16[32,1,1024]{2,1,0:T(2,128)(2,1)S(1)} %get-tuple-element.9), kind=kOutput, calls=%fused_computation.8 | convolution fusion | flops 117440512 | bytes 3964928 | tf_op jit(solution)/shard_map/dot_general | solution.py:50
  49.0 2.7 %fusion = f32[32,1792]{1,0:T(8,128)S(1)} fusion(bf16[3,1024,1792]{2,1,0:T(8,128)(2,1)} %bitcast.61, bf16[32,1,1024]{2,1,0:T(2,128)(2,1)S(1)} %get-tuple-element.10), kind=kOutput, calls=%fused_computation.2 | convolution fusion | flops 117440512 | bytes 3964928 | tf_op jit(solution)/shard_map/dot_general | solution.py:51
  51.8 0.9 pad_maximum_fusion.1
  52.7 0.0 all-gather.7.cloned.1.call-update
  52.7 0.0 all-gather.5.cloned.1.call-start
  52.7 0.2 reshape_reshape.3
  52.9 0.1 convert_reduce_fusion.1
  53.0 26.0 %all-gather.7.cloned.1.call-done = f32[64,5376]{1,0:T(8,128)} async-done(((f32[32,5376]{1,0:T(8,128)}), f32[64,5376]{1,0:T(8,128)}) %all-gather.7.cloned.1.call-update) | async-done | bytes 1376272 | tf_op jit(solution)/shard_map/all_gather | solution.py:55
  79.0 1.5 %reduce_sum.66 = f32[32,5376]{1,0:T(8,128)S(1)} reduce(f32[2,32,5376]{2,1,0:T(8,128)} %bitcast.64, f32[]{:T(128)} %constant.10.clone.1), dimensions={0}, to_apply=%region_4.5 | reduce | flops 172032 | bytes 2064388 | tf_op jit(solution)/shard_map/reduce_sum | solution.py:56
  80.5 0.2 multiply_convert_fusion
  80.8 0.8 pad_maximum_fusion.2
  81.5 0.0 all-gather.5.cloned.1.call-update
  81.5 0.3 constant_dynamic-slice_fusion.1
  81.8 0.1 copy.63
  81.9 7.1 %all_to_all.14 = bf16[4,32,512]{2,1,0:T(8,128)(2,1)S(1)} all-to-all(bf16[4,32,512]{2,1,0:T(8,128)(2,1)S(1)} %bitcast.66), channel_id=1, replica_groups=mesh['rep'=4,'ep'=4,'grp'=2] {'rep'}, dimensions={0} | all-to-all | bytes 262144 | tf_op jit(solution)/shard_map/all_to_all | solution.py:44
  89.1 0.0 copy-start.1
  89.1 3.2 %fusion.1 = f32[32,1024]{1,0:T(8,128)S(1)} fusion(bf16[32,1792]{1,0:T(8,128)(2,1)S(1)} %get-tuple-element.7, bf16[3,1024,1792]{2,1,0:T(8,128)(2,1)} %bitcast.62), kind=kOutput, calls=%fused_computation.5 | convolution fusion | flops 117440512 | bytes 3915776 | tf_op jit(solution)/shard_map/dot_general | solution.py:68
  92.3 3.2 %fusion.6 = bf16[32,1024]{1,0:T(8,128)(2,1)S(1)} fusion(f32[32,1024]{1,0:T(8,128)S(1)} %fusion.1, bf16[32,1792]{1,0:T(8,128)(2,1)S(1)} %get-tuple-element.6, bf16[3,1024,1792]{2,1,0:T(8,128)(2,1)} %bitcast.63), kind=kOutput, calls=%fused_computation.16 | convolution fusion | flops 117506048 | bytes 3981312 | tf_op jit(solution)/shard_map/dot_general | solution.py:69
  95.6 0.1 broadcast_in_dim.5
  95.7 0.7 all_to_all.9
  96.3 4.9 %all-to-all-start = ((bf16[8,4,1152]{2,1,0:T(4,128)(2,1)}), bf16[8,4,1152]{2,1,0:T(4,128)(2,1)S(1)}, u32[]{:S(2)}, u32[]{:S(2)}) async-start(bf16[8,4,1152]{2,1,0:T(4,128)(2,1)} %all_to_all.9), calls=%async_computation | async-start | bytes 147456 | tf_op jit(solution)/shard_map/all_to_all | solution.py:71
  101.2 0.2 fusion.32
  101.4 6.9 %all-to-all-done = bf16[8,4,1152]{2,1,0:T(4,128)(2,1)S(1)} async-done(((bf16[8,4,1152]{2,1,0:T(4,128)(2,1)}), bf16[8,4,1152]{2,1,0:T(4,128)(2,1)S(1)}, u32[]{:S(2)}, u32[]{:S(2)}) %all-to-all-start) | async-done | bytes 73760 | tf_op jit(solution)/shard_map/all_to_all | solution.py:71
  108.3 0.1 slice_reduce_fusion
  108.4 0.1 fusion.19
  108.5 0.0 copy-done.1
  108.5 0.6 broadcast_select_fusion
  109.1 1.8 %convolution_convert_fusion = bf16[128,2048]{1,0:T(8,128)(2,1)} fusion(f32[4,2048]{1,0:T(4,128)S(1)} %bitcast.67, f32[128]{0:T(128)S(1)} %get-tuple-element.3, f32[128]{0:T(128)S(1)} %sub.10), kind=kOutput, calls=%fused_computation.12 | convolution fusion | flops 12846080 | bytes 558080 | tf_op jit(solution)/shard_map/dot_general | solution.py:78
  110.9 0.0 all-gather.5.cloned.1.call-done
  110.9 1.4 %convolution_bitcast_fusion.1 = f32[256,1,1792]{2,0,1:T(8,128)S(1)} fusion(bf16[128,5376]{1,0:T(8,128)(2,1)} %all-gather.5.cloned.1.call-done, bf16[128,1,256]{2,1,0:T(2,128)(2,1)S(1)} %get-tuple-element.11), kind=kOutput, calls=%fused_computation.10 | convolution fusion | flops 117440512 | bytes 2359296 | tf_op jit(solution)/shard_map/dot_general | solution.py:82
  112.4 1.4 %convolution_bitcast_fusion.2 = f32[256,1,1792]{2,0,1:T(8,128)S(1)} fusion(bf16[128,5376]{1,0:T(8,128)(2,1)} %all-gather.5.cloned.1.call-done, bf16[128,1,256]{2,1,0:T(2,128)(2,1)S(1)} %get-tuple-element.11), kind=kOutput, calls=%fused_computation.11 | convolution fusion | flops 117440512 | bytes 2359296 | tf_op jit(solution)/shard_map/dot_general | solution.py:82
  113.8 1.4 %convolution_bitcast_fusion = f32[256,1,1792]{2,0,1:T(8,128)S(1)} fusion(bf16[128,5376]{1,0:T(8,128)(2,1)} %all-gather.5.cloned.1.call-done, bf16[128,1,256]{2,1,0:T(2,128)(2,1)S(1)} %get-tuple-element.12), kind=kOutput, calls=%fused_computation.9 | convolution fusion | flops 117440512 | bytes 2359296 | tf_op jit(solution)/shard_map/dot_general | solution.py:82
  115.2 2.8 %pad_maximum_fusion = f32[256,3,1792]{2,0,1:T(8,128)} fusion(f32[256,1,1792]{2,0,1:T(8,128)S(1)} %convolution_bitcast_fusion, f32[256,1,1792]{2,0,1:T(8,128)S(1)} %convolution_bitcast_fusion.1, f32[256,1,1792]{2,0,1:T(8,128)S(1)} %convolution_bitcast_fusion.2), kind=kLoop, calls=%fused_computation | loop fusion | flops 2752512 | bytes 11010048 | tf_op jit(solution)/shard_map/stack | solution.py:87
  (8 shorter events, 0.1 us)
Async XLA Ops:
  7.2 1.3 %copy-start = (bf16[128,2048]{1,0:T(8,128)(2,1)S(1)}, bf16[128,2048]{1,0:T(8,128)(2,1)}, u32[]{:S(2)}) copy-start(bf16[128,2048]{1,0:T(8,128)(2,1)} %param.6) | copy-start | bytes 1572868
  7.2 71.8 %all-gather.7.cloned.1.call-start = ((), (), s32[]{:S(2)}) async-start(), calls=%async_computation.3 | async-start | bytes 2064384 | tf_op jit(solution)/shard_map/all_gather | solution.py:55
  52.7 58.2 %all-gather.5.cloned.1.call-start = ((), (), s32[]{:S(2)}) async-start(), calls=%async_computation.2 | async-start | bytes 1720320 | tf_op jit(solution)/shard_map/all_gather | solution.py:66
  89.1 19.4 %copy-start.1 = (s32[128,2]{0,1:T(2,128)S(1)}, s32[128,2]{0,1:T(2,128)}, u32[]{:S(2)}) copy-start(s32[128,2]{0,1:T(2,128)} %param.7) | copy-start | bytes 3076
  96.3 11.9 %all-to-all-start = ((bf16[8,4,1152]{2,1,0:T(4,128)(2,1)}), bf16[8,4,1152]{2,1,0:T(4,128)(2,1)S(1)}, u32[]{:S(2)}, u32[]{:S(2)}) async-start(bf16[8,4,1152]{2,1,0:T(4,128)(2,1)} %all_to_all.9), calls=%async_computation | async-start | bytes 147456 | tf_op jit(solution)/shard_map/all_to_all | solution.py:71
Sparse Core Ops, SparseCore 0:
  52.8 26.1 all-gather.6
  81.7 18.5 all-gather.4
